TPU v7x, 32 devices: a whole 2x2x4 slice. The times are simulated.
32 devices in a mesh: groups: 1, wide: 32 (over z, y, x, core).
Axes of the slice: x: 2, y: 2, z: 4, core: 2. Of those that a mesh axis runs over, the one named last changes fastest.
Arguments:
- queries: bfloat16 [2, 1024, 4096], P('groups', 'wide'), may hold values from -100 to 100
- key_rows: bfloat16 [2, 1024, 1024], P('groups', 'wide'), may hold values from -5 to 5
- value_rows: bfloat16 [2, 1024, 1024], P('groups', 'wide'), may hold values from -5 to 5
- residual: bfloat16 [2, 1024, 4096], P('groups', 'wide'), may hold values from -4 to 4
- segment_ids: int32 [2048], P('groups'), may hold values from 0 to 47, never falling along the last dimension, each value on 1 to 64 neighbouring positions
- routes: int32 [2, 1024, 2], P('groups', 'wide'), may hold values from 0 to 15, all different within a row; in each aligned block of 32 rows (0 to 31, 32 to 63, ..., all dimensions but the last counted through in order) at most 5 rows name the same one
- route_weights: float32 [2, 1024, 2], P('groups', 'wide'), may hold values from 0.1 to 1
- norm_gain: float32 [4096], replicated, may hold values from 0.5 to 1.5
- norm_bias: float32 [4096], replicated, may hold values from -3 to 3
- w_gate: bfloat16 [4096, 51200], P(None, 'wide'), may hold values from -0.09375 to 0.09375
- w_up: bfloat16 [4096, 51200], P(None, 'wide'), may hold values from -0.09375 to 0.09375
- w_down: bfloat16 [51200, 4096], P('wide'), may hold values from -0.109375 to 0.109375
Outputs:
- layer_out: bfloat16 [2, 1024, 4096], P('groups', 'wide')
Inputs may be any that keep to these rules, and one draw needn't show every extreme that they name: `routes`: the 2 experts of a row differ. In each micro-batch, no expert is named more than 5 times by the rows of one device, and in every draw some expert is named exactly 5 times by one device's rows. `segment_ids`: never falls along the positions; no document has more than 64 positions, and one has exactly 64.
All inputs are finite; a program needn't handle non-finite values.
Results may differ from a plain program's by a relative error of at most 0.012.
Values may be sent and summed in bfloat16 or wider, within the bound.
A program may use at most 128 MiB of HBM per device.

v0:
```python
import functools
import math

import jax
import jax.numpy as jnp
from jax import lax
from jax.experimental import pallas as pl
from jax.experimental.pallas import tpu as pltpu
from jax.sharding import PartitionSpec as P

HEADS = 32
KVH = 8
HD = 128
EXPERTS = 16
TOP = 2
C = 5


def passed_along(x, axis, by):
    length = lax.axis_size(axis)
    return lax.ppermute(x, axis, [(i, (i + by) % length) for i in range(length)])


def slot_targets(flat):
    onehot = (flat[..., None] == jnp.arange(EXPERTS, dtype=jnp.int32)).astype(jnp.int32)
    rank = jnp.cumsum(onehot, axis=-2) - 1
    slot = jnp.sum(onehot * rank, axis=-1)
    return flat * C + slot


UNITS_MOST = 400
VMEM_BYTES = 48 * 1024 * 1024
VMEM_MOST = 63 * 1024 * 1024


def tile_of(size):
    fits = [t for t in range(16, UNITS_MOST + 1, 16) if size % t == 0]
    return fits[-1] if fits else size


def expert_kernel(parts, *refs):
    row_refs = refs[:parts]
    gate_ref, up_ref, down_ref = refs[parts : parts + 3]
    out_refs = refs[parts + 3 : 2 * parts + 3]
    total = refs[2 * parts + 3]
    step = pl.program_id(0)
    last = pl.num_programs(0) - 1
    by_rows = (((1,), (1,)), ((), ()))
    rows = jnp.concatenate([ref[...] for ref in row_refs], axis=0)
    gate = lax.dot_general(rows, gate_ref[...], by_rows, preferred_element_type=jnp.float32)
    upward = lax.dot_general(rows, up_ref[...], by_rows, preferred_element_type=jnp.float32)
    hidden = (gate / (1.0 + jnp.exp(-gate)) * upward).astype(jnp.bfloat16)
    count = rows.shape[0] // parts
    added = jnp.dot(hidden, down_ref[...], preferred_element_type=jnp.float32)

    @pl.when(step == 0)
    def _():
        total[...] = added

    @pl.when(step > 0)
    def _():
        total[...] += added

    @pl.when(step == last)
    def _():
        for part in range(parts):
            block = total[part * count : (part + 1) * count, :]
            out_refs[part][...] = block.astype(jnp.bfloat16)


def compute_expert(row_parts, w_gate, w_up, w_down):
    parts = len(row_parts)
    count, width = row_parts[0].shape
    units = w_gate.shape[1]
    tile = tile_of(units)
    total = parts * count
    row_spec = pl.BlockSpec((count, width), lambda i: (0, 0))
    weight_spec = pl.BlockSpec((tile, width), lambda i: (i, 0))
    return pl.pallas_call(
        functools.partial(expert_kernel, parts),
        grid=(units // tile,),
        in_specs=[row_spec] * parts + [weight_spec] * 3,
        out_specs=[row_spec] * parts,
        out_shape=[jax.ShapeDtypeStruct((count, width), jnp.bfloat16)] * parts,
        scratch_shapes=[pltpu.VMEM((total, width), jnp.float32)],
        compiler_params=pltpu.CompilerParams(vmem_limit_bytes=VMEM_BYTES),
        cost_estimate=pl.CostEstimate(
            flops=6 * total * width * units,
            bytes_accessed=6 * width * units + 4 * total * width,
            transcendentals=total * units,
        ),
        name="expert",
    )(*row_parts, w_gate.T, w_up.T, w_down)


def shards(
    queries,
    key_rows,
    value_rows,
    residual,
    segment_ids,
    routes,
    route_weights,
    norm_gain,
    norm_bias,
    w_gate,
    w_up,
    w_down,
):
    wide_count = lax.axis_size("wide")
    device_index = lax.axis_index("wide")
    micro_count, tok_local, width = queries.shape
    tokens_micro = tok_local * wide_count
    doc_longest = micro_count * tokens_micro // 32
    scale = 1.0 / math.sqrt(HD)
    reach = doc_longest // tok_local
    group = HEADS // KVH
    steps_back = list(range(reach, 0, -1))
    received = []
    for step in steps_back:
        received.append(passed_along((key_rows, value_rows), "wide", step))
    span = (reach + 1) * tok_local
    before = jnp.full((reach * tok_local,), -1, jnp.int32)
    segments = jnp.concatenate([before, segment_ids])
    key_place = jnp.arange(span, dtype=jnp.int32) - reach * tok_local
    causal = key_place[None, :] <= jnp.arange(tok_local, dtype=jnp.int32)[:, None]
    results = []
    for local_micro in range(micro_count):
        earlier = max(local_micro - 1, 0)
        key_parts = []
        value_parts = []
        for position, step in enumerate(steps_back):
            key_far, value_far = received[position]
            crossed = device_index < step
            key_parts.append(jnp.where(crossed, key_far[earlier], key_far[local_micro]))
            value_parts.append(jnp.where(crossed, value_far[earlier], value_far[local_micro]))
        key_parts.append(key_rows[local_micro])
        value_parts.append(value_rows[local_micro])
        window_keys = jnp.concatenate(key_parts, axis=0)
        window_values = jnp.concatenate(value_parts, axis=0)
        key_seg = lax.dynamic_slice(
            segments, (local_micro * tokens_micro + device_index * tok_local,), (span,)
        )
        query_seg = key_seg[reach * tok_local :]
        allowed = (key_seg[None, :] == query_seg[:, None]) & causal
        query_now = queries[local_micro].reshape(tok_local, KVH, group, HD)
        scores = (
            jnp.einsum(
                "tkgd,skd->kgts",
                query_now,
                window_keys.reshape(span, KVH, HD),
                preferred_element_type=jnp.float32,
            )
            * scale
        )
        scores = jnp.where(allowed[None, None], scores, -1e30)
        top = jnp.max(scores, axis=3, keepdims=True)
        expo = jnp.exp(scores - top)
        probs = (expo / jnp.sum(expo, axis=3, keepdims=True)).astype(jnp.bfloat16)
        result = jnp.einsum(
            "kgts,skd->tkgd",
            probs,
            window_values.reshape(span, KVH, HD),
            preferred_element_type=jnp.float32,
        ).astype(jnp.bfloat16)
        results.append(result.reshape(tok_local, width))
    team = wide_count // EXPERTS
    across = [[e * team + r for e in range(EXPERTS)] for r in range(team)]
    inside = [[e * team + r for r in range(team)] for e in range(EXPERTS)]
    swap = [(i, i ^ 1) for i in range(wide_count)]
    fold = (width // 128, 128)
    slots = EXPERTS * C

    def exchanged(x):
        sent = x.reshape(EXPERTS, C, *fold)
        return lax.all_to_all(sent, "wide", 0, 0, axis_index_groups=across, tiled=True)

    state = []
    for micro in range(micro_count):
        mixed = residual[micro].astype(jnp.float32) + results[micro].astype(jnp.float32)
        center = mixed - jnp.mean(mixed, axis=-1, keepdims=True)
        variance = jnp.mean(center * center, axis=-1, keepdims=True)
        normed = (center / jnp.sqrt(variance + 1e-05) * norm_gain + norm_bias).astype(
            jnp.bfloat16
        )
        target = slot_targets(routes[micro].reshape(tok_local * TOP)).reshape(tok_local, TOP)
        hits = target[..., None] == jnp.arange(slots, dtype=jnp.int32)
        chooser = jnp.any(hits, axis=1).astype(jnp.bfloat16)
        packed = jnp.einsum(
            "te,td->ed", chooser, normed, preferred_element_type=jnp.float32
        ).astype(jnp.bfloat16)
        state.append((mixed, hits, exchanged(packed).reshape(slots, *fold)))
    outputs = []
    for micro in range(micro_count):
        mixed, hits, landed = state[micro]
        if team == 2:
            other = lax.ppermute(landed, "wide", swap)
            pair = (landed.reshape(slots, width), other.reshape(slots, width))
            mine, theirs = compute_expert(pair, w_gate, w_up, w_down)
            theirs = lax.ppermute(theirs, "wide", swap)
            summed = mine.astype(jnp.float32) + theirs.astype(jnp.float32)
        else:
            rows = lax.all_gather(landed, "wide", axis_index_groups=inside, tiled=True)
            rows = rows.reshape(team * slots, width)
            (partial_value,) = compute_expert((rows,), w_gate, w_up, w_down)
            blocks = lax.all_to_all(
                partial_value.reshape(team, slots, *fold),
                "wide",
                0,
                0,
                axis_index_groups=inside,
                tiled=True,
            )
            summed = blocks.astype(jnp.float32).sum(axis=0).reshape(slots, width)
        returned = exchanged(summed.astype(jnp.bfloat16)).reshape(slots, width)
        shares = jnp.sum(jnp.where(hits, route_weights[micro][..., None], 0.0), axis=1)
        high = shares.astype(jnp.bfloat16)
        low = (shares - high.astype(jnp.float32)).astype(jnp.bfloat16)
        mixture = jnp.dot(high, returned, preferred_element_type=jnp.float32) + jnp.dot(
            low, returned, preferred_element_type=jnp.float32
        )
        outputs.append((mixed + mixture).astype(jnp.bfloat16))
    return jnp.stack(outputs)


MESH_ID = pl.DeviceIdType.MESH


def flipped(place, by, bits):
    total = 0
    for bit in range(bits):
        own = (place // (1 << bit)) % 2
        total = total + ((own + (by >> bit) % 2) % 2) * (1 << bit)
    return total


def column_of(row):
    size = row.shape[1]
    down = lax.broadcasted_iota(jnp.int32, (size, size), 0)
    across = lax.broadcasted_iota(jnp.int32, (size, size), 1)
    spread = jnp.broadcast_to(row, (size, size))
    return jnp.sum(jnp.where(down == across, spread, 0.0), axis=1, keepdims=True)


def layer_kernel(
    sizes,
    seg_ref,
    routes_ref,
    shares_ref,
    gain_ref,
    bias_ref,
    q_hbm,
    k_hbm,
    v_hbm,
    res_hbm,
    gate_hbm,
    up_hbm,
    down_hbm,
    out_ref,
    q_buf,
    k_win,
    v_win,
    res_buf,
    gate_buf,
    up_buf,
    down_buf,
    mixed,
    normed,
    fold,
    send_buf,
    mine_buf,
    theirs_buf,
    rows_buf,
    hidden,
    part_own,
    part_send,
    part_recv,
    ret_buf,
    ret_recv,
    load_sem,
    weight_sem,
    kv_send,
    kv_recv,
    out_send,
    out_recv,
    pass_send,
    pass_recv,
    part_ssem,
    part_rsem,
    ret_send,
    ret_rsem,
):
    count, micros, tok, width, reach = sizes
    chips = count // 2
    bits = chips.bit_length() - 1
    lanes = width // 128
    slots = EXPERTS * C
    block = C * lanes
    group = HEADS // KVH
    span = (reach + 1) * tok
    units = gate_hbm.shape[0]
    me = lax.axis_index("wide")
    chip = me // 2
    core = me % 2
    partner = chip * 2 + (1 - core)
    order = list(range(chips - 1, 0, -1))

    def peer(k):
        return flipped(chip, k, bits) * 2 + core

    def to(device):
        return dict(device_id={"wide": device}, device_id_type=MESH_ID)

    loads = [
        pltpu.make_async_copy(q_hbm, q_buf, load_sem.at[0]),
        pltpu.make_async_copy(res_hbm, res_buf, load_sem.at[1]),
    ]
    for m in range(micros):
        own = pl.ds(reach * tok, tok)
        loads.append(pltpu.make_async_copy(k_hbm.at[m], k_win.at[m, own], load_sem.at[2 + 2 * m]))
        loads.append(pltpu.make_async_copy(v_hbm.at[m], v_win.at[m, own], load_sem.at[3 + 2 * m]))
    for load in loads:
        load.start()

    barrier = pltpu.get_barrier_semaphore()

    def greet(step, carry):
        pl.semaphore_signal(barrier, inc=1, **to((me + step) % count))
        return carry

    lax.fori_loop(1, count, greet, 0)
    pl.semaphore_wait(barrier, count - 1)

    kv_copies = {}
    for m in range(micros):
        for step in range(1, reach + 1):
            crossed = (me + step) // count
            source = (m + micros - crossed) % micros
            window = pl.ds((reach - step) * tok, tok)
            target = (me + step) % count
            for which, (far, win) in enumerate(((k_hbm, k_win), (v_hbm, v_win))):
                copy = pltpu.make_async_remote_copy(
                    far.at[source],
                    win.at[m, window],
                    kv_send.at[m, step - 1, which],
                    kv_recv.at[m, step - 1, which],
                    **to(target),
                )
                copy.start()
                kv_copies[m, step, which] = copy

    weight_loads = [
        pltpu.make_async_copy(far, near, weight_sem.at[i])
        for i, (far, near) in enumerate(
            ((gate_hbm, gate_buf), (up_hbm, up_buf), (down_hbm, down_buf))
        )
    ]
    for load in weight_loads:
        load.start()

    def allowed_of(m):
        start = m * tok * count + me * tok - reach * tok
        rows = seg_ref.shape[0]
        first = (start + rows * 128) // 128
        both = jnp.concatenate(
            [seg_ref[pl.ds(first % rows, 1), :], seg_ref[pl.ds((first + 1) % rows, 1), :]],
            axis=1,
        )
        shift = (start + rows * 128) % 128
        seg = both[:, 0:span]
        for skip in range(tok, 128, tok):
            picked = (jnp.zeros((1, span), jnp.int32) + shift) == skip
            seg = jnp.where(picked, both[:, skip : skip + span], seg)
        seg = seg.astype(jnp.float32)
        query_seg = column_of(seg[:, reach * tok :])
        place = lax.broadcasted_iota(jnp.int32, (tok, span), 1)
        now = lax.broadcasted_iota(jnp.int32, (tok, span), 0)
        fits = jnp.broadcast_to(seg, (tok, span)) == jnp.broadcast_to(query_seg, (tok, span))
        fits = fits & (place <= now + reach * tok) & (place + start >= 0)
        return jnp.concatenate([jnp.where(fits, 1.0, 0.0)] * group, axis=0)

    def slot_maps(m):
        names = routes_ref[m].astype(jnp.float32)
        row_names = [names[i : i + 1, :] for i in range(TOP)]
        col_names = [column_of(row) for row in row_names]
        weights = [column_of(shares_ref[m][i : i + 1, :]) for i in range(TOP)]
        before = lax.broadcasted_iota(jnp.int32, (tok, tok), 0)
        after = lax.broadcasted_iota(jnp.int32, (tok, tok), 1)

        def slot_rows(i):
            total = jnp.zeros((tok, tok), jnp.float32)
            for other in range(TOP):
                same = (col_names[other] == row_names[i]) & (before < after)
                total = total + jnp.where(same, 1.0, 0.0)
            return jnp.sum(total, axis=0, keepdims=True)

        def slot_cols(i):
            total = jnp.zeros((tok, tok), jnp.float32)
            for other in range(TOP):
                same = (row_names[other] == col_names[i]) & (after < before)
                total = total + jnp.where(same, 1.0, 0.0)
            return jnp.sum(total, axis=1, keepdims=True)

        def places(shape, axis):
            at = lax.broadcasted_iota(jnp.int32, shape, axis)
            turn = jnp.zeros(shape, jnp.int32)
            for k in range(1, EXPERTS):
                turn = turn + jnp.where(at >= k * C, 1, 0)
            expert = jnp.bitwise_xor(turn, jnp.zeros(shape, jnp.int32) + chip)
            return expert.astype(jnp.float32), (at - turn * C).astype(jnp.float32)

        expert, slot = places((slots, tok), 0)
        chooser = jnp.zeros((slots, tok), jnp.float32)
        for i in range(TOP):
            chooser = chooser + jnp.where(
                (expert == row_names[i]) & (slot == slot_rows(i)), 1.0, 0.0
            )
        expert, slot = places((tok, slots), 1)
        parts = jnp.zeros((tok, slots), jnp.float32)
        for i in range(TOP):
            parts = parts + jnp.where(
                (expert == col_names[i]) & (slot == slot_cols(i)), weights[i], 0.0
            )
        high = parts.astype(jnp.bfloat16)
        low = (parts - high.astype(jnp.float32)).astype(jnp.bfloat16)
        return chooser.astype(jnp.bfloat16), jnp.concatenate([high, low], axis=0)

    by_rows = (((1,), (1,)), ((), ()))
    scale = 1.0 / math.sqrt(HD)

    def attend(m, allowed):
        for head in range(KVH):
            cols = slice(head * HD, (head + 1) * HD)
            first = head * group
            queries = jnp.concatenate(
                [q_buf[m, :, (first + g) * HD : (first + g + 1) * HD] for g in range(group)],
                axis=0,
            )
            scores = lax.dot_general(
                queries, k_win[m, :, cols], by_rows, preferred_element_type=jnp.float32
            )
            scores = jnp.where(allowed > 0.5, scores * scale, -1e30)
            expo = jnp.exp(scores - jnp.max(scores, axis=1, keepdims=True))
            probs = (expo / jnp.sum(expo, axis=1, keepdims=True)).astype(jnp.bfloat16)
            result = jnp.dot(probs, v_win[m, :, cols], preferred_element_type=jnp.float32)
            result = result.astype(jnp.bfloat16).astype(jnp.float32)
            for g in range(group):
                at = slice((first + g) * HD, (first + g + 1) * HD)
                mixed[m, :, at] = (
                    res_buf[m, :, at].astype(jnp.float32) + result[g * tok : (g + 1) * tok, :]
                )

    def normalize(m):
        values = mixed[m]
        center = values - jnp.mean(values, axis=1, keepdims=True)
        variance = jnp.mean(center * center, axis=1, keepdims=True)
        scaled = center * (1.0 / jnp.sqrt(variance + 1e-05))
        normed[...] = (scaled * gain_ref[...] + bias_ref[...]).astype(jnp.bfloat16)

    chunk = min(512, width)
    per_chunk = chunk // 128

    def pack(m, chooser):
        for j in range(width // chunk):
            packed = jnp.dot(
                chooser, normed[:, j * chunk : (j + 1) * chunk], preferred_element_type=jnp.float32
            )
            for i in range(per_chunk):
                fold[pl.ds(j * per_chunk + i, slots, stride=lanes), :] = packed[
                    :, i * 128 : (i + 1) * 128
                ]
        for k in order + [0]:
            send_buf[m, k] = fold[k * block : (k + 1) * block, :].astype(jnp.bfloat16)

    def exchange(m, k, source, target, ssem, rsem, device):
        return pltpu.make_async_remote_copy(
            source.at[m, k], target.at[m, k], ssem.at[m, k], rsem.at[m, k], **to(device)
        )

    def sent(m, k):
        return exchange(m, k, send_buf, mine_buf, out_send, out_recv, peer(k))

    def passed(m, k):
        source = mine_buf if k else send_buf
        return exchange(m, k, source, theirs_buf, pass_send, pass_recv, partner)

    def returned(m, k):
        return exchange(m, k, ret_buf, ret_recv, ret_send, ret_rsem, peer(k))

    def swapped(m, j):
        return exchange(m, j, part_send, part_recv, part_ssem, part_rsem, partner)

    def first_half(m, allowed, chooser):
        for step in range(1, reach + 1):
            for which in range(2):
                kv_copies[m, step, which].wait_recv()
        if m == 0:
            for load in loads:
                load.wait()
        attend(m, allowed)
        normalize(m)
        pack(m, chooser)
        for k in order:
            sent(m, k).start()
        passed(m, 0).start()

    def lay_rows(at):
        for j in range(lanes):
            rows_buf[at : at + slots, j * 128 : (j + 1) * 128] = fold[
                pl.ds(j, slots, stride=lanes), :
            ].astype(jnp.bfloat16)

    def gather_rows(m):
        fold[0:block, :] = send_buf[m, 0].astype(jnp.float32)
        for k in order:
            sent(m, k).wait_recv()
            passed(m, k).start()
            fold[k * block : (k + 1) * block, :] = mine_buf[m, k].astype(jnp.float32)
        lay_rows(0)
        for k in [0] + order:
            passed(m, k).wait_recv()
            fold[k * block : (k + 1) * block, :] = theirs_buf[m, k].astype(jnp.float32)
        lay_rows(slots)

    tile = 256
    whole_tiles = units // tile

    def hidden_tile(start, size):
        rows = rows_buf[...]
        at = pl.ds(start, size)
        gate = lax.dot_general(
            rows, gate_buf[at, :], by_rows, preferred_element_type=jnp.float32
        )
        upward = lax.dot_general(
            rows, up_buf[at, :], by_rows, preferred_element_type=jnp.float32
        )
        hidden[:, at] = (gate / (1.0 + jnp.exp(-gate)) * upward).astype(jnp.bfloat16)

    def experts(m):
        def hidden_step(i, carry):
            hidden_tile(pl.multiple_of(i * tile, tile), tile)
            return carry

        lax.fori_loop(0, whole_tiles, hidden_step, 0)
        if units % tile:
            hidden_tile(whole_tiles * tile, units % tile)

        def down_step(j, carry):
            at = pl.ds(pl.multiple_of(j * chunk, chunk), chunk)
            added = jnp.dot(hidden[...], down_buf[:, at], preferred_element_type=jnp.float32)
            added = added.astype(jnp.bfloat16)
            part_own[j] = added[0:slots, :]
            part_send[m, j] = added[slots : 2 * slots, :]
            swapped(m, j).start()
            return carry

        lax.fori_loop(0, width // chunk, down_step, 0)

    def give_back(m):
        for j in range(width // chunk):
            swapped(m, j).wait_recv()
            total = part_own[j].astype(jnp.float32) + part_recv[m, j].astype(jnp.float32)
            for i in range(per_chunk):
                fold[pl.ds(j * per_chunk + i, slots, stride=lanes), :] = total[
                    :, i * 128 : (i + 1) * 128
                ]
        for k in order + [0]:
            ret_buf[m, k] = fold[k * block : (k + 1) * block, :].astype(jnp.bfloat16)
        for k in order:
            returned(m, k).start()

    def combine(m, parts):
        fold[0:block, :] = ret_buf[m, 0].astype(jnp.float32)
        for k in order:
            returned(m, k).wait_recv()
            fold[k * block : (k + 1) * block, :] = ret_recv[m, k].astype(jnp.float32)
        for j in range(width // chunk):
            pieces = [
                fold[pl.ds(j * per_chunk + i, slots, stride=lanes), :].astype(jnp.bfloat16)
                for i in range(per_chunk)
            ]
            both = jnp.dot(
                parts, jnp.concatenate(pieces, axis=1), preferred_element_type=jnp.float32
            )
            at = slice(j * chunk, (j + 1) * chunk)
            out_ref[m, :, at] = (mixed[m, :, at] + (both[0:tok] + both[tok : 2 * tok])).astype(
                jnp.bfloat16
            )

    masks = [allowed_of(m) for m in range(micros)]
    maps = [slot_maps(m) for m in range(micros)]
    for m in range(micros):
        first_half(m, masks[m], maps[m][0])
    for m in range(micros):
        gather_rows(m)
        if m == 0:
            for load in weight_loads:
                load.wait()
        experts(m)
        give_back(m)
    for m in range(micros):
        combine(m, maps[m][1])
    for m in range(micros):
        for step in range(1, reach + 1):
            for which in range(2):
                kv_copies[m, step, which].wait_send()
        for k in order:
            sent(m, k).wait_send()
            returned(m, k).wait_send()
        for k in [0] + order:
            passed(m, k).wait_send()
        for j in range(width // chunk):
            swapped(m, j).wait_send()


def whole_layer(
    queries,
    key_rows,
    value_rows,
    residual,
    segment_ids,
    routes,
    route_weights,
    norm_gain,
    norm_bias,
    w_gate,
    w_up,
    w_down,
):
    count = lax.axis_size("wide")
    micros, tok, width = queries.shape
    reach = micros * tok * count // 32 // tok
    kv_width = key_rows.shape[2]
    units = w_gate.shape[1]
    chips = count // 2
    slots = EXPERTS * C
    lanes = width // 128
    block = C * lanes
    span = (reach + 1) * tok
    chunk = min(512, width)
    chunks = width // chunk
    near = pl.BlockSpec(memory_space=pltpu.VMEM)
    far = pl.BlockSpec(memory_space=pl.ANY)
    half = jnp.bfloat16
    full = jnp.float32
    exchange = pltpu.VMEM((micros, chips, block, 128), half)
    weight = pltpu.VMEM((units, width), half)
    dma = pltpu.SemaphoreType.DMA
    scratch = [
        pltpu.VMEM((micros, tok, width), half),
        pltpu.VMEM((micros, span, kv_width), half),
        pltpu.VMEM((micros, span, kv_width), half),
        pltpu.VMEM((micros, tok, width), half),
        weight,
        weight,
        weight,
        pltpu.VMEM((micros, tok, width), full),
        pltpu.VMEM((tok, width), half),
        pltpu.VMEM((slots * lanes, 128), full),
        exchange,
        exchange,
        exchange,
        pltpu.VMEM((2 * slots, width), half),
        pltpu.VMEM((2 * slots, units), half),
        pltpu.VMEM((chunks, slots, chunk), half),
        pltpu.VMEM((micros, chunks, slots, chunk), half),
        pltpu.VMEM((micros, chunks, slots, chunk), half),
        exchange,
        exchange,
        dma((2 + 2 * micros,)),
        dma((3,)),
        dma((micros, reach, 2)),
        dma((micros, reach, 2)),
        dma((micros, chips)),
        dma((micros, chips)),
        dma((micros, chips)),
        dma((micros, chips)),
        dma((micros, chunks)),
        dma((micros, chunks)),
        dma((micros, chips)),
        dma((micros, chips)),
    ]
    return pl.pallas_call(
        functools.partial(layer_kernel, (count, micros, tok, width, reach)),
        out_shape=jax.ShapeDtypeStruct((micros, tok, width), half),
        in_specs=[near] * 5 + [far] * 7,
        out_specs=near,
        scratch_shapes=scratch,
        compiler_params=pltpu.CompilerParams(
            collective_id=0, has_side_effects=True, vmem_limit_bytes=VMEM_MOST
        ),
        name="layer",
    )(
        segment_ids.reshape(-1, 128),
        jnp.transpose(routes, (0, 2, 1)),
        jnp.transpose(route_weights, (0, 2, 1)),
        norm_gain.reshape(1, width),
        norm_bias.reshape(1, width),
        queries,
        key_rows,
        value_rows,
        residual,
        w_gate.T,
        w_up.T,
        w_down,
    )


def solution(mesh):
    placed = (
        P("groups", "wide", None),
        P("groups", "wide", None),
        P("groups", "wide", None),
        P("groups", "wide", None),
        P("groups"),
        P("groups", "wide", None),
        P("groups", "wide", None),
        P(),
        P(),
        P(None, "wide"),
        P(None, "wide"),
        P("wide", None),
    )
    wide_count = mesh.shape["wide"]
    paired = wide_count == 2 * EXPERTS

    def layer(*args):
        return whole_layer(*args) if paired else shards(*args)

    return jax.shard_map(
        layer, mesh=mesh, in_specs=placed, out_specs=P("groups", "wide", None), check_vma=False
    )
```

profile of v0, /device:TPU:0, one launch (start us, length us, event | category | flops | bytes accessed | tf_op | source)
XLA Modules:
  0.0 93.8 jit_solution(9995311274585384843)
XLA Ops:
  0.0 91.9 %layer.1 = bf16[2,32,4096]{2,1,0:T(8,128)(2,1)} custom-call(s32[16,128]{1,0:T(8,128)} %bitcast.11, s32[2,2,32]{2,1,0:T(2,128)} %bitcast.12, f32[2,2,32]{2,1,0:T(2,128)} %bitcast.13, f32[1,4096]{1,0:T(1,128)} %bitcast.9, f32[1,4096]{1,0:T(1,128)} %bitcast.10, bf16[2,32,4096]{2,1,0:T(8,128)(2,1)} %q_hbm.1, bf16[2,32,1024]{2,1,0:T(8,128)(2,1)} %k_hbm.1, ...), custom_call_target="tpu_custom_call" | custom-call | tf_op jit(solution)/shard_map/layer/pallas_call | solution.py:683
  91.9 1.9 %copy.14 = bf16[2,32,4096]{2,1,0:T(8,128)(2,1)} copy(bf16[2,32,4096]{2,1,0:T(8,128)(2,1)} %layer.1) | data formatting | bytes 1048576
where the time goes:
time: 94.6 us; the launch traced here: 93.8 us
  Pallas kernels  91.9 us (97%)
  local copies, waits for them, and re-layouts  1.87 us (2%)
    pallas_call x1, Pallas kernels, whole_layer(): pl.pallas_call(functools.partial(layer_kernel, (count, micros, tok, width...  91.9 us

commit v1 on v0

--- a/solution.py
+++ b/solution.py
@@ -30,7 +30,7 @@
 
 UNITS_MOST = 400
 VMEM_BYTES = 48 * 1024 * 1024
-VMEM_MOST = 63 * 1024 * 1024
+VMEM_MOST = 56 * 1024 * 1024
 
 
 def tile_of(size):
@@ -329,6 +329,76 @@
         return carry
 
     lax.fori_loop(1, count, greet, 0)
+
+    def allowed_of(m):
+        start = m * tok * count + me * tok - reach * tok
+        rows = seg_ref.shape[0]
+        first = (start + rows * 128) // 128
+        both = jnp.concatenate(
+            [seg_ref[pl.ds(first % rows, 1), :], seg_ref[pl.ds((first + 1) % rows, 1), :]],
+            axis=1,
+        )
+        shift = (start + rows * 128) % 128
+        seg = both[:, 0:span]
+        for skip in range(tok, 128, tok):
+            picked = (jnp.zeros((1, span), jnp.int32) + shift) == skip
+            seg = jnp.where(picked, both[:, skip : skip + span], seg)
+        seg = seg.astype(jnp.float32)
+        query_seg = column_of(seg[:, reach * tok :])
+        place = lax.broadcasted_iota(jnp.int32, (tok, span), 1)
+        now = lax.broadcasted_iota(jnp.int32, (tok, span), 0)
+        fits = jnp.broadcast_to(seg, (tok, span)) == jnp.broadcast_to(query_seg, (tok, span))
+        fits = fits & (place <= now + reach * tok) & (place + start >= 0)
+        return jnp.concatenate([jnp.where(fits, 1.0, 0.0)] * group, axis=0)
+
+    def slot_maps(m):
+        names = routes_ref[m].astype(jnp.float32)
+        row_names = [names[i : i + 1, :] for i in range(TOP)]
+        col_names = [column_of(row) for row in row_names]
+        weights = [column_of(shares_ref[m][i : i + 1, :]) for i in range(TOP)]
+        before = lax.broadcasted_iota(jnp.int32, (tok, tok), 0)
+        after = lax.broadcasted_iota(jnp.int32, (tok, tok), 1)
+
+        def slot_rows(i):
+            total = jnp.zeros((tok, tok), jnp.float32)
+            for other in range(TOP):
+                same = (col_names[other] == row_names[i]) & (before < after)
+                total = total + jnp.where(same, 1.0, 0.0)
+            return jnp.sum(total, axis=0, keepdims=True)
+
+        def slot_cols(i):
+            total = jnp.zeros((tok, tok), jnp.float32)
+            for other in range(TOP):
+                same = (row_names[other] == col_names[i]) & (after < before)
+                total = total + jnp.where(same, 1.0, 0.0)
+            return jnp.sum(total, axis=1, keepdims=True)
+
+        def places(shape, axis):
+            at = lax.broadcasted_iota(jnp.int32, shape, axis)
+            turn = jnp.zeros(shape, jnp.int32)
+            for k in range(1, EXPERTS):
+                turn = turn + jnp.where(at >= k * C, 1, 0)
+            expert = jnp.bitwise_xor(turn, jnp.zeros(shape, jnp.int32) + chip)
+            return expert.astype(jnp.float32), (at - turn * C).astype(jnp.float32)
+
+        expert, slot = places((slots, tok), 0)
+        chooser = jnp.zeros((slots, tok), jnp.float32)
+        for i in range(TOP):
+            chooser = chooser + jnp.where(
+                (expert == row_names[i]) & (slot == slot_rows(i)), 1.0, 0.0
+            )
+        expert, slot = places((tok, slots), 1)
+        parts = jnp.zeros((tok, slots), jnp.float32)
+        for i in range(TOP):
+            parts = parts + jnp.where(
+                (expert == col_names[i]) & (slot == slot_cols(i)), weights[i], 0.0
+            )
+        high = parts.astype(jnp.bfloat16)
+        low = (parts - high.astype(jnp.float32)).astype(jnp.bfloat16)
+        return chooser.astype(jnp.bfloat16), jnp.concatenate([high, low], axis=0)
+
+    masks = [allowed_of(m) for m in range(micros)]
+    maps = [slot_maps(m) for m in range(micros)]
     pl.semaphore_wait(barrier, count - 1)
 
     kv_copies = {}
@@ -358,97 +428,44 @@
     for load in weight_loads:
         load.start()
 
-    def allowed_of(m):
-        start = m * tok * count + me * tok - reach * tok
-        rows = seg_ref.shape[0]
-        first = (start + rows * 128) // 128
-        both = jnp.concatenate(
-            [seg_ref[pl.ds(first % rows, 1), :], seg_ref[pl.ds((first + 1) % rows, 1), :]],
-            axis=1,
-        )
-        shift = (start + rows * 128) % 128
-        seg = both[:, 0:span]
-        for skip in range(tok, 128, tok):
-            picked = (jnp.zeros((1, span), jnp.int32) + shift) == skip
-            seg = jnp.where(picked, both[:, skip : skip + span], seg)
-        seg = seg.astype(jnp.float32)
-        query_seg = column_of(seg[:, reach * tok :])
-        place = lax.broadcasted_iota(jnp.int32, (tok, span), 1)
-        now = lax.broadcasted_iota(jnp.int32, (tok, span), 0)
-        fits = jnp.broadcast_to(seg, (tok, span)) == jnp.broadcast_to(query_seg, (tok, span))
-        fits = fits & (place <= now + reach * tok) & (place + start >= 0)
-        return jnp.concatenate([jnp.where(fits, 1.0, 0.0)] * group, axis=0)
-
-    def slot_maps(m):
-        names = routes_ref[m].astype(jnp.float32)
-        row_names = [names[i : i + 1, :] for i in range(TOP)]
-        col_names = [column_of(row) for row in row_names]
-        weights = [column_of(shares_ref[m][i : i + 1, :]) for i in range(TOP)]
-        before = lax.broadcasted_iota(jnp.int32, (tok, tok), 0)
-        after = lax.broadcasted_iota(jnp.int32, (tok, tok), 1)
-
-        def slot_rows(i):
-            total = jnp.zeros((tok, tok), jnp.float32)
-            for other in range(TOP):
-                same = (col_names[other] == row_names[i]) & (before < after)
-                total = total + jnp.where(same, 1.0, 0.0)
-            return jnp.sum(total, axis=0, keepdims=True)
-
-        def slot_cols(i):
-            total = jnp.zeros((tok, tok), jnp.float32)
-            for other in range(TOP):
-                same = (row_names[other] == col_names[i]) & (after < before)
-                total = total + jnp.where(same, 1.0, 0.0)
-            return jnp.sum(total, axis=1, keepdims=True)
-
-        def places(shape, axis):
-            at = lax.broadcasted_iota(jnp.int32, shape, axis)
-            turn = jnp.zeros(shape, jnp.int32)
-            for k in range(1, EXPERTS):
-                turn = turn + jnp.where(at >= k * C, 1, 0)
-            expert = jnp.bitwise_xor(turn, jnp.zeros(shape, jnp.int32) + chip)
-            return expert.astype(jnp.float32), (at - turn * C).astype(jnp.float32)
-
-        expert, slot = places((slots, tok), 0)
-        chooser = jnp.zeros((slots, tok), jnp.float32)
-        for i in range(TOP):
-            chooser = chooser + jnp.where(
-                (expert == row_names[i]) & (slot == slot_rows(i)), 1.0, 0.0
-            )
-        expert, slot = places((tok, slots), 1)
-        parts = jnp.zeros((tok, slots), jnp.float32)
-        for i in range(TOP):
-            parts = parts + jnp.where(
-                (expert == col_names[i]) & (slot == slot_cols(i)), weights[i], 0.0
-            )
-        high = parts.astype(jnp.bfloat16)
-        low = (parts - high.astype(jnp.float32)).astype(jnp.bfloat16)
-        return chooser.astype(jnp.bfloat16), jnp.concatenate([high, low], axis=0)
-
     by_rows = (((1,), (1,)), ((), ()))
     scale = 1.0 / math.sqrt(HD)
 
     def attend(m, allowed):
-        for head in range(KVH):
-            cols = slice(head * HD, (head + 1) * HD)
-            first = head * group
-            queries = jnp.concatenate(
-                [q_buf[m, :, (first + g) * HD : (first + g + 1) * HD] for g in range(group)],
-                axis=0,
-            )
-            scores = lax.dot_general(
-                queries, k_win[m, :, cols], by_rows, preferred_element_type=jnp.float32
-            )
-            scores = jnp.where(allowed > 0.5, scores * scale, -1e30)
-            expo = jnp.exp(scores - jnp.max(scores, axis=1, keepdims=True))
-            probs = (expo / jnp.sum(expo, axis=1, keepdims=True)).astype(jnp.bfloat16)
-            result = jnp.dot(probs, v_win[m, :, cols], preferred_element_type=jnp.float32)
-            result = result.astype(jnp.bfloat16).astype(jnp.float32)
-            for g in range(group):
-                at = slice((first + g) * HD, (first + g + 1) * HD)
-                mixed[m, :, at] = (
-                    res_buf[m, :, at].astype(jnp.float32) + result[g * tok : (g + 1) * tok, :]
+        together = KVH // 2
+        for start in range(0, KVH, together):
+            heads = range(start, start + together)
+            cols = [slice(head * HD, (head + 1) * HD) for head in heads]
+            scores = []
+            for head, at in zip(heads, cols):
+                queries = [
+                    q_buf[m, :, (head * group + g) * HD : (head * group + g + 1) * HD]
+                    for g in range(group)
+                ]
+                scores.append(
+                    lax.dot_general(
+                        jnp.concatenate(queries, axis=0),
+                        k_win[m, :, at],
+                        by_rows,
+                        preferred_element_type=jnp.float32,
+                    )
                 )
+            scores = [jnp.where(allowed > 0.5, score * scale, -1e30) for score in scores]
+            tops = [jnp.max(score, axis=1, keepdims=True) for score in scores]
+            expos = [jnp.exp(score - top) for score, top in zip(scores, tops)]
+            sums = [jnp.sum(expo, axis=1, keepdims=True) for expo in expos]
+            probs = [(expo / total).astype(jnp.bfloat16) for expo, total in zip(expos, sums)]
+            results = [
+                jnp.dot(prob, v_win[m, :, at], preferred_element_type=jnp.float32)
+                for prob, at in zip(probs, cols)
+            ]
+            for head, result in zip(heads, results):
+                result = result.astype(jnp.bfloat16).astype(jnp.float32)
+                for g in range(group):
+                    at = slice((head * group + g) * HD, (head * group + g + 1) * HD)
+                    mixed[m, :, at] = (
+                        res_buf[m, :, at].astype(jnp.float32) + result[g * tok : (g + 1) * tok, :]
+                    )
 
     def normalize(m):
         values = mixed[m]
@@ -457,7 +474,7 @@
         scaled = center * (1.0 / jnp.sqrt(variance + 1e-05))
         normed[...] = (scaled * gain_ref[...] + bias_ref[...]).astype(jnp.bfloat16)
 
-    chunk = min(512, width)
+    chunk = min(1024, width)
     per_chunk = chunk // 128
 
     def pack(m, chooser):
@@ -500,8 +517,9 @@
         attend(m, allowed)
         normalize(m)
         pack(m, chooser)
-        for k in order:
-            sent(m, k).start()
+        if m == 0:
+            for k in order:
+                sent(m, k).start()
         passed(m, 0).start()
 
     def lay_rows(at):
@@ -515,6 +533,8 @@
         for k in order:
             sent(m, k).wait_recv()
             passed(m, k).start()
+            if m + 1 < micros:
+                sent(m + 1, k).start()
             fold[k * block : (k + 1) * block, :] = mine_buf[m, k].astype(jnp.float32)
         lay_rows(0)
         for k in [0] + order:
@@ -522,8 +542,7 @@
             fold[k * block : (k + 1) * block, :] = theirs_buf[m, k].astype(jnp.float32)
         lay_rows(slots)
 
-    tile = 256
-    whole_tiles = units // tile
+    tile = tile_of(units)
 
     def hidden_tile(start, size):
         rows = rows_buf[...]
@@ -537,24 +556,15 @@
         hidden[:, at] = (gate / (1.0 + jnp.exp(-gate)) * upward).astype(jnp.bfloat16)
 
     def experts(m):
-        def hidden_step(i, carry):
-            hidden_tile(pl.multiple_of(i * tile, tile), tile)
-            return carry
-
-        lax.fori_loop(0, whole_tiles, hidden_step, 0)
-        if units % tile:
-            hidden_tile(whole_tiles * tile, units % tile)
-
-        def down_step(j, carry):
-            at = pl.ds(pl.multiple_of(j * chunk, chunk), chunk)
+        for i in range(units // tile):
+            hidden_tile(i * tile, tile)
+        for j in range(width // chunk):
+            at = slice(j * chunk, (j + 1) * chunk)
             added = jnp.dot(hidden[...], down_buf[:, at], preferred_element_type=jnp.float32)
             added = added.astype(jnp.bfloat16)
             part_own[j] = added[0:slots, :]
             part_send[m, j] = added[slots : 2 * slots, :]
             swapped(m, j).start()
-            return carry
-
-        lax.fori_loop(0, width // chunk, down_step, 0)
 
     def give_back(m):
         for j in range(width // chunk):
@@ -587,8 +597,6 @@
                 jnp.bfloat16
             )
 
-    masks = [allowed_of(m) for m in range(micros)]
-    maps = [slot_maps(m) for m in range(micros)]
     for m in range(micros):
         first_half(m, masks[m], maps[m][0])
     for m in range(micros):
@@ -637,7 +645,7 @@
     lanes = width // 128
     block = C * lanes
     span = (reach + 1) * tok
-    chunk = min(512, width)
+    chunk = min(1024, width)
     chunks = width // chunk
     near = pl.BlockSpec(memory_space=pltpu.VMEM)
     far = pl.BlockSpec(memory_space=pl.ANY)

time: 94.6 us -> 83.3 us (0.88)
  Pallas kernels: 91.9 us -> 80.7 us
    pallas_call x1, Pallas kernels: 91.9 us -> 80.7 us  [whole_layer(): pl.pallas_call(functools.partial(layer_kernel, (count, micros, tok, width...]
where the time goes in v1:
time: 83.3 us; the launch traced here: 82.6 us
  Pallas kernels  80.7 us (97%)
  local copies, waits for them, and re-layouts  1.87 us (2%)
    pallas_call x1, Pallas kernels, whole_layer(): pl.pallas_call(functools.partial(layer_kernel, (count, micros, tok, width...  80.7 us
    unnamed x1, local copies, waits for them, and re-layouts  1.87 us

profile of v1, /device:TPU:0, one launch (start us, length us, event | category | flops | bytes accessed | tf_op | source)
XLA Modules:
  0.0 82.6 jit_solution(13985811878395071837)
XLA Ops:
  0.0 80.7 %layer.1 = bf16[2,32,4096]{2,1,0:T(8,128)(2,1)} custom-call(s32[16,128]{1,0:T(8,128)} %bitcast.11, s32[2,2,32]{2,1,0:T(2,128)} %bitcast.12, f32[2,2,32]{2,1,0:T(2,128)} %bitcast.13, f32[1,4096]{1,0:T(1,128)} %bitcast.9, f32[1,4096]{1,0:T(1,128)} %bitcast.10, bf16[2,32,4096]{2,1,0:T(8,128)(2,1)} %q_hbm.1, bf16[2,32,1024]{2,1,0:T(8,128)(2,1)} %k_hbm.1, ...), custom_call_target="tpu_custom_call" | custom-call | tf_op jit(solution)/shard_map/layer/pallas_call | solution.py:691
  80.7 1.9 %copy.14 = bf16[2,32,4096]{2,1,0:T(8,128)(2,1)} copy(bf16[2,32,4096]{2,1,0:T(8,128)(2,1)} %layer.1) | data formatting | bytes 1048576

commit v2 on v1

--- a/solution.py
+++ b/solution.py
@@ -269,7 +269,6 @@
     fold,
     send_buf,
     mine_buf,
-    theirs_buf,
     rows_buf,
     hidden,
     part_own,
@@ -373,8 +372,8 @@
                 total = total + jnp.where(same, 1.0, 0.0)
             return jnp.sum(total, axis=1, keepdims=True)
 
-        def places(shape, axis):
-            at = lax.broadcasted_iota(jnp.int32, shape, axis)
+        def places(shape, axis, low=0):
+            at = lax.broadcasted_iota(jnp.int32, shape, axis) + low
             turn = jnp.zeros(shape, jnp.int32)
             for k in range(1, EXPERTS):
                 turn = turn + jnp.where(at >= k * C, 1, 0)
@@ -387,38 +386,44 @@
             chooser = chooser + jnp.where(
                 (expert == row_names[i]) & (slot == slot_rows(i)), 1.0, 0.0
             )
-        expert, slot = places((tok, slots), 1)
-        parts = jnp.zeros((tok, slots), jnp.float32)
-        for i in range(TOP):
-            parts = parts + jnp.where(
-                (expert == col_names[i]) & (slot == slot_cols(i)), weights[i], 0.0
-            )
-        high = parts.astype(jnp.bfloat16)
-        low = (parts - high.astype(jnp.float32)).astype(jnp.bfloat16)
-        return chooser.astype(jnp.bfloat16), jnp.concatenate([high, low], axis=0)
+        halves = []
+        for low in (0, slots // 2):
+            expert, slot = places((tok, slots // 2), 1, low)
+            parts = jnp.zeros((tok, slots // 2), jnp.float32)
+            for i in range(TOP):
+                parts = parts + jnp.where(
+                    (expert == col_names[i]) & (slot == slot_cols(i)), weights[i], 0.0
+                )
+            high = parts.astype(jnp.bfloat16)
+            rest = (parts - high.astype(jnp.float32)).astype(jnp.bfloat16)
+            halves.append(jnp.concatenate([high, rest], axis=0))
+        return chooser.astype(jnp.bfloat16), halves
 
     masks = [allowed_of(m) for m in range(micros)]
     maps = [slot_maps(m) for m in range(micros)]
     pl.semaphore_wait(barrier, count - 1)
 
-    kv_copies = {}
-    for m in range(micros):
+    def neighbour(m, step, which):
+        far, win = ((k_hbm, k_win), (v_hbm, v_win))[which]
+        crossed = (me + step) // count
+        return pltpu.make_async_remote_copy(
+            far.at[(m + micros - crossed) % micros],
+            win.at[m, pl.ds((reach - step) * tok, tok)],
+            kv_send.at[m, step - 1, which],
+            kv_recv.at[m, step - 1, which],
+            **to((me + step) % count),
+        )
+
+    def send_window(m):
+        for which in range(2):
+            for step in range(1, reach + 1):
+                neighbour(m, step, which).start()
+
+    def await_window(m, which):
         for step in range(1, reach + 1):
-            crossed = (me + step) // count
-            source = (m + micros - crossed) % micros
-            window = pl.ds((reach - step) * tok, tok)
-            target = (me + step) % count
-            for which, (far, win) in enumerate(((k_hbm, k_win), (v_hbm, v_win))):
-                copy = pltpu.make_async_remote_copy(
-                    far.at[source],
-                    win.at[m, window],
-                    kv_send.at[m, step - 1, which],
-                    kv_recv.at[m, step - 1, which],
-                    **to(target),
-                )
-                copy.start()
-                kv_copies[m, step, which] = copy
-
+            neighbour(m, step, which).wait_recv()
+
+    send_window(0)
     weight_loads = [
         pltpu.make_async_copy(far, near, weight_sem.at[i])
         for i, (far, near) in enumerate(
@@ -454,6 +459,8 @@
             tops = [jnp.max(score, axis=1, keepdims=True) for score in scores]
             expos = [jnp.exp(score - top) for score, top in zip(scores, tops)]
             sums = [jnp.sum(expo, axis=1, keepdims=True) for expo in expos]
+            if start == 0:
+                await_window(m, 1)
             probs = [(expo / total).astype(jnp.bfloat16) for expo, total in zip(expos, sums)]
             results = [
                 jnp.dot(prob, v_win[m, :, at], preferred_element_type=jnp.float32)
@@ -497,9 +504,15 @@
     def sent(m, k):
         return exchange(m, k, send_buf, mine_buf, out_send, out_recv, peer(k))
 
-    def passed(m, k):
-        source = mine_buf if k else send_buf
-        return exchange(m, k, source, theirs_buf, pass_send, pass_recv, partner)
+    def passed(m, j):
+        cols = pl.ds(j * chunk, chunk)
+        return pltpu.make_async_remote_copy(
+            rows_buf.at[m, pl.ds(0, slots), cols],
+            rows_buf.at[m, pl.ds(slots, slots), cols],
+            pass_send.at[m, j],
+            pass_recv.at[m, j],
+            **to(partner),
+        )
 
     def returned(m, k):
         return exchange(m, k, ret_buf, ret_recv, ret_send, ret_rsem, peer(k))
@@ -508,9 +521,9 @@
         return exchange(m, j, part_send, part_recv, part_ssem, part_rsem, partner)
 
     def first_half(m, allowed, chooser):
-        for step in range(1, reach + 1):
-            for which in range(2):
-                kv_copies[m, step, which].wait_recv()
+        await_window(m, 0)
+        if m + 1 < micros:
+            send_window(m + 1)
         if m == 0:
             for load in loads:
                 load.wait()
@@ -520,32 +533,31 @@
         if m == 0:
             for k in order:
                 sent(m, k).start()
-        passed(m, 0).start()
-
-    def lay_rows(at):
-        for j in range(lanes):
-            rows_buf[at : at + slots, j * 128 : (j + 1) * 128] = fold[
-                pl.ds(j, slots, stride=lanes), :
-            ].astype(jnp.bfloat16)
+
+    lag = chips // 2 - 2
 
     def gather_rows(m):
         fold[0:block, :] = send_buf[m, 0].astype(jnp.float32)
-        for k in order:
+        waiting = list(order)
+        for turn, k in enumerate(order):
             sent(m, k).wait_recv()
-            passed(m, k).start()
-            if m + 1 < micros:
+            if m + 1 < micros and turn >= lag:
+                sent(m + 1, waiting.pop(0)).start()
+            fold[k * block : (k + 1) * block, :] = mine_buf[m, k].astype(jnp.float32)
+        if m + 1 < micros:
+            for k in waiting:
                 sent(m + 1, k).start()
-            fold[k * block : (k + 1) * block, :] = mine_buf[m, k].astype(jnp.float32)
-        lay_rows(0)
-        for k in [0] + order:
-            passed(m, k).wait_recv()
-            fold[k * block : (k + 1) * block, :] = theirs_buf[m, k].astype(jnp.float32)
-        lay_rows(slots)
+        for j in range(width // chunk):
+            for i in range(j * per_chunk, (j + 1) * per_chunk):
+                rows_buf[m, 0:slots, i * 128 : (i + 1) * 128] = fold[
+                    pl.ds(i, slots, stride=lanes), :
+                ].astype(jnp.bfloat16)
+            passed(m, j).start()
 
     tile = tile_of(units)
 
-    def hidden_tile(start, size):
-        rows = rows_buf[...]
+    def hidden_tile(m, start, size):
+        rows = rows_buf[m]
         at = pl.ds(start, size)
         gate = lax.dot_general(
             rows, gate_buf[at, :], by_rows, preferred_element_type=jnp.float32
@@ -555,9 +567,13 @@
         )
         hidden[:, at] = (gate / (1.0 + jnp.exp(-gate)) * upward).astype(jnp.bfloat16)
 
-    def experts(m):
+    def upward_half(m):
+        for j in range(width // chunk):
+            passed(m, j).wait_recv()
         for i in range(units // tile):
-            hidden_tile(i * tile, tile)
+            hidden_tile(m, i * tile, tile)
+
+    def downward_half(m):
         for j in range(width // chunk):
             at = slice(j * chunk, (j + 1) * chunk)
             added = jnp.dot(hidden[...], down_buf[:, at], preferred_element_type=jnp.float32)
@@ -579,46 +595,61 @@
         for k in order:
             returned(m, k).start()
 
+    def mixture(parts, low, rows, j):
+        pieces = [
+            fold[pl.ds(low * lanes + j * per_chunk + i, rows, stride=lanes), :]
+            for i in range(per_chunk)
+        ]
+        pieces = [piece.astype(jnp.bfloat16) for piece in pieces]
+        both = jnp.dot(parts, jnp.concatenate(pieces, axis=1), preferred_element_type=jnp.float32)
+        return both[0:tok] + both[tok : 2 * tok]
+
     def combine(m, parts):
-        fold[0:block, :] = ret_buf[m, 0].astype(jnp.float32)
-        for k in order:
-            returned(m, k).wait_recv()
-            fold[k * block : (k + 1) * block, :] = ret_recv[m, k].astype(jnp.float32)
+        middle = slots // 2
+        for turn, k in enumerate(order + [0]):
+            if k:
+                returned(m, k).wait_recv()
+                landed = ret_recv[m, k]
+            else:
+                landed = ret_buf[m, 0]
+            fold[k * block : (k + 1) * block, :] = landed.astype(jnp.float32)
+            if turn + 1 == chips // 2:
+                for j in range(width // chunk):
+                    at = slice(j * chunk, (j + 1) * chunk)
+                    mixed[m, :, at] = mixed[m, :, at] + mixture(parts[1], middle, middle, j)
         for j in range(width // chunk):
-            pieces = [
-                fold[pl.ds(j * per_chunk + i, slots, stride=lanes), :].astype(jnp.bfloat16)
-                for i in range(per_chunk)
-            ]
-            both = jnp.dot(
-                parts, jnp.concatenate(pieces, axis=1), preferred_element_type=jnp.float32
-            )
             at = slice(j * chunk, (j + 1) * chunk)
-            out_ref[m, :, at] = (mixed[m, :, at] + (both[0:tok] + both[tok : 2 * tok])).astype(
+            out_ref[m, :, at] = (mixed[m, :, at] + mixture(parts[0], 0, middle, j)).astype(
                 jnp.bfloat16
             )
 
     for m in range(micros):
         first_half(m, masks[m], maps[m][0])
+    gather_rows(0)
+    for load in weight_loads:
+        load.wait()
     for m in range(micros):
-        gather_rows(m)
-        if m == 0:
-            for load in weight_loads:
-                load.wait()
-        experts(m)
+        upward_half(m)
+        downward_half(m)
         give_back(m)
+        if m + 1 < micros:
+            gather_rows(m + 1)
     for m in range(micros):
+        if m + 1 == micros:
+            for i in range(micros):
+                for step in range(1, reach + 1):
+                    for which in range(2):
+                        neighbour(i, step, which).wait_send()
+                for k in order:
+                    sent(i, k).wait_send()
+                    if i < m:
+                        returned(i, k).wait_send()
+                for j in range(width // chunk):
+                    passed(i, j).wait_send()
+                    swapped(i, j).wait_send()
         combine(m, maps[m][1])
-    for m in range(micros):
-        for step in range(1, reach + 1):
-            for which in range(2):
-                kv_copies[m, step, which].wait_send()
-        for k in order:
-            sent(m, k).wait_send()
-            returned(m, k).wait_send()
-        for k in [0] + order:
-            passed(m, k).wait_send()
-        for j in range(width // chunk):
-            swapped(m, j).wait_send()
+    for k in order:
+        returned(micros - 1, k).wait_send()
 
 
 def whole_layer(
@@ -667,8 +698,7 @@
         pltpu.VMEM((slots * lanes, 128), full),
         exchange,
         exchange,
-        exchange,
-        pltpu.VMEM((2 * slots, width), half),
+        pltpu.VMEM((micros, 2 * slots, width), half),
         pltpu.VMEM((2 * slots, units), half),
         pltpu.VMEM((chunks, slots, chunk), half),
         pltpu.VMEM((micros, chunks, slots, chunk), half),
@@ -681,8 +711,8 @@
         dma((micros, reach, 2)),
         dma((micros, chips)),
         dma((micros, chips)),
-        dma((micros, chips)),
-        dma((micros, chips)),
+        dma((micros, chunks)),
+        dma((micros, chunks)),
         dma((micros, chunks)),
         dma((micros, chunks)),
         dma((micros, chips)),
@@ -690,7 +720,7 @@
     ]
     return pl.pallas_call(
         functools.partial(layer_kernel, (count, micros, tok, width, reach)),
-        out_shape=jax.ShapeDtypeStruct((micros, tok, width), half),
+        out_shape=pltpu.VMEM((micros, tok, width), half),
         in_specs=[near] * 5 + [far] * 7,
         out_specs=near,
         scratch_shapes=scratch,

time: 83.3 us -> 79.4 us (0.953)
  Pallas kernels: 80.7 us -> 78.3 us
  local copies, waits for them, and re-layouts: 1.87 us -> 0.8 us
    pallas_call x1, Pallas kernels: 80.7 us -> 78.3 us  [whole_layer(): pl.pallas_call(functools.partial(layer_kernel, (count, micros, tok, width...]
    unnamed x1, local copies, waits for them, and re-layouts: 1.87 us -> 0.8 us
where the time goes in v2:
time: 79.4 us; the launch traced here: 79.1 us
  Pallas kernels  78.3 us (99%)
  local copies, waits for them, and re-layouts  0.8 us (1%)
    pallas_call x1, Pallas kernels, whole_layer(): pl.pallas_call(functools.partial(layer_kernel, (count, micros, tok, width...  78.3 us

profile of v2, /device:TPU:0, one launch (start us, length us, event | category | flops | bytes accessed | tf_op | source)
XLA Modules:
  0.0 79.1 jit_solution(2005624517873137940)
XLA Ops:
  0.0 78.3 %layer.1 = bf16[2,32,4096]{2,1,0:T(8,128)(2,1)S(1)} custom-call(s32[16,128]{1,0:T(8,128)} %bitcast.11, s32[2,2,32]{2,1,0:T(2,128)} %bitcast.12, f32[2,2,32]{2,1,0:T(2,128)} %bitcast.13, f32[1,4096]{1,0:T(1,128)} %bitcast.9, f32[1,4096]{1,0:T(1,128)} %bitcast.10, bf16[2,32,4096]{2,1,0:T(8,128)(2,1)} %q_hbm.1, bf16[2,32,1024]{2,1,0:T(8,128)(2,1)} %k_hbm.1, ...), custom_call_target="tpu_custom_call" | custom-call | tf_op jit(solution)/shard_map/layer/pallas_call | solution.py:721
  78.3 0.8 %copy.14 = bf16[2,32,4096]{2,1,0:T(8,128)(2,1)} copy(bf16[2,32,4096]{2,1,0:T(8,128)(2,1)S(1)} %layer.1) | data formatting | bytes 1048576
